TPU v7x, 256 devices: a whole 4x4x8 slice. The times are simulated.
256 devices in a mesh: tm: 16 (over y, x), space: 2 (over core), head: 8 (over z).
Axes of the slice: x: 4, y: 4, z: 8, core: 2. Of those that a mesh axis runs over, the one named last changes fastest.
Arguments:
- query: bfloat16 [16, 8, 80, 5120], P('tm', 'space', None, 'head'), may hold values from -5 to 5
- key: bfloat16 [16, 8, 80, 5120], P('tm', 'space', None, 'head'), may hold values from -5 to 5
- value: bfloat16 [16, 8, 80, 5120], P('tm', 'space', None, 'head'), may hold values from -6 to 6
- window: int32 [16, 16], replicated, may hold values from -1 to 4, as said below
- out_weight: bfloat16 [5120, 5120], P('head'), may hold values from -0.078125 to 0.078125
Outputs:
- projected: bfloat16 [16, 8, 80, 5120], P('tm', 'space', None, 'head')
Inputs may be any that keep to these rules, and one draw needn't show every extreme that they name: window[f, f] = 4 for every frame f.
All inputs are finite; a program needn't handle non-finite values.
Results may differ from a plain program's by a relative error of at most 0.023.
Values may be sent and summed in bfloat16 or wider, within the bound.
A program may use at most 128 MiB of HBM per device.

v0:
```python
import math
import jax
import jax.numpy as jnp
from jax import lax
from jax.sharding import PartitionSpec as P

HD = 128
HALO = 4
NEG_FILL = -1e30


def padded_2(x, sides, width):
    for axis, dim in sides:
        size, length = (lax.axis_size(axis), x.shape[dim])
        up = [(i, (i + 1) % size) for i in range(size - 1)]
        down = [(j, i) for i, j in up]
        last = lax.slice_in_dim(x, length - width, length, axis=dim)
        first = lax.slice_in_dim(x, 0, width, axis=dim)
        before = lax.ppermute(last, axis, up)
        after = lax.ppermute(first, axis, down)
        x = jnp.concatenate([before, x, after], axis=dim)
    return x


def frame_mask(widths, query_rows, key_rows, total_rows, width):
    count = widths.shape[0]
    distance = jnp.abs(query_rows[:, None] - key_rows[None, :])
    inside_grid = (key_rows >= 0) & (key_rows < total_rows)
    inside = (
        (widths[:, None, None] >= 0)
        & (distance[None] <= widths[:, None, None])
        & inside_grid[None, None, :]
    )
    span_rows = key_rows.shape[0]
    full = jnp.broadcast_to(
        inside[:, :, None, :, None], (count, query_rows.shape[0], width, span_rows, width)
    )
    return full.reshape(count * query_rows.shape[0] * width, span_rows * width)


def absorb(state, queries, keys, values, mask):
    run_max, run_sum, run_acc = state
    scale = 1.0 / math.sqrt(HD)
    scores = jnp.einsum("qhd,khd->hqk", queries, keys, preferred_element_type=jnp.float32) * scale
    new_max = jnp.maximum(run_max, jnp.max(jnp.where(mask[None], scores, NEG_FILL), axis=-1))
    weights = jnp.where(mask[None], jnp.exp(scores - new_max[..., None]), 0.0)
    factor = jnp.exp(run_max - new_max)
    new_sum = run_sum * factor + jnp.sum(weights, axis=-1)
    new_acc = run_acc * factor[..., None] + jnp.einsum(
        "hqk,khd->hqd", weights.astype(jnp.bfloat16), values, preferred_element_type=jnp.float32
    )
    return (new_max, new_sum, new_acc)


def absorb_frame(state, queries, widths, kv_frame, query_rows, key_rows, total_rows):
    span_rows, width, feats = (kv_frame.shape[1], kv_frame.shape[2], kv_frame.shape[3])
    heads_dev = feats // HD
    keys = kv_frame[0].reshape(span_rows * width, heads_dev, HD)
    values = kv_frame[1].reshape(span_rows * width, heads_dev, HD)
    mask = frame_mask(widths, query_rows, key_rows, total_rows, width)
    return absorb(state, queries, keys, values, mask)


def empty_state(heads_dev, count):
    return (
        jnp.full((heads_dev, count), NEG_FILL, jnp.float32),
        jnp.zeros((heads_dev, count), jnp.float32),
        jnp.zeros((heads_dev, count, HD), jnp.float32),
    )


def body(query, key, value, window, out_weight):
    frames_dev, rows_dev, width, feats = query.shape
    heads_dev = feats // HD
    qcount = frames_dev * rows_dev * width
    total_rows = rows_dev * lax.axis_size("space")
    first_row = lax.axis_index("space") * rows_dev
    first_frame = lax.axis_index("tm") * frames_dev
    query_rows = first_row + jnp.arange(rows_dev, dtype=jnp.int32)
    stacked = jnp.stack([key, value])
    padded = padded_2(stacked, (("space", 2),), HALO)
    key_rows = first_row - HALO + jnp.arange(rows_dev + 2 * HALO, dtype=jnp.int32)
    my_windows = lax.dynamic_slice_in_dim(window, first_frame, frames_dev, 0)
    queries = query.reshape(qcount, heads_dev, HD)
    piece = lax.all_gather(padded, "tm", axis=1, tiled=True)

    def one_frame(carry, offset):
        kv_frame = lax.dynamic_index_in_dim(piece, offset, 1, False)
        widths = lax.dynamic_index_in_dim(my_windows, offset, 1, False)
        return (
            absorb_frame(carry, queries, widths, kv_frame, query_rows, key_rows, total_rows),
            None,
        )

    result, unused = lax.scan(
        one_frame, empty_state(heads_dev, qcount), jnp.arange(piece.shape[1], dtype=jnp.int32)
    )
    run_max, run_sum, run_acc = result
    attended = (
        (run_acc / run_sum[..., None])
        .transpose(1, 0, 2)
        .reshape(qcount, feats)
        .astype(jnp.bfloat16)
    )
    share_rows = out_weight.shape[1] // lax.axis_size("head")
    mixed = lax.psum_scatter(
        lax.dot_general(
            out_weight, attended, (((0,), (1,)), ((), ())), preferred_element_type=jnp.float32
        ).astype(jnp.bfloat16),
        "head",
        scatter_dimension=0,
        tiled=True,
    ).astype(jnp.float32)
    return mixed.T.reshape(frames_dev, rows_dev, width, share_rows).astype(jnp.bfloat16)


def solution(mesh):
    placed = (
        P("tm", "space", None, "head"),
        P("tm", "space", None, "head"),
        P("tm", "space", None, "head"),
        P(),
        P("head", None),
    )
    return jax.shard_map(
        body, mesh=mesh, in_specs=placed, out_specs=P("tm", "space", None, "head"), check_vma=False
    )
```

profile of v0, /device:TPU:1, one launch (start us, length us, event | category | flops | bytes accessed | tf_op | source)
XLA Modules:
  0.0 810.0 jit_solution(69779024183798448)
XLA Ops:
  21.1 230.9 %all-gather.2.cloned.1.call-done = bf16[2,16,12,80,640]{4,3,2,1,0:T(8,128)(2,1)} async-done(((bf16[2,1,12,80,640]{4,3,2,1,0:T(8,128)(2,1)}), bf16[2,16,12,80,640]{4,3,2,1,0:T(8,128)(2,1)}) %all-gather.2.cloned.1.call-update) | async-done | bytes 39321616 | tf_op jit(solution)/shard_map/all_gather | solution.py:85
  252.0 484.5 %while.15 = (s32[]{:T(128)}, f32[5,320]{1,0:T(8,128)S(1)}, f32[5,320]{1,0:T(8,128)}, f32[5,320,128]{2,1,0:T(8,128)}, s32[16]{0:T(128)S(1)}, /*index=5*/s32[1,16]...) while((s32[]{:T(128)}, f32[5,320]{1,0:T(8,128)S(1)}, ...), condition=%wide.region_3.4_spmd.clone, body=%wide.region_0.3_spmd.clone.sunk | while | flops 803950720 | bytes 35329148 | solution.py:95
  263.2 5.7 fusion.43
  292.7 5.7 fusion.43
  306.1 5.7 fusion.46
  323.1 5.7 fusion.43
  336.5 5.7 fusion.46
  353.4 5.7 fusion.43
  366.8 5.7 fusion.46
  383.7 5.7 fusion.43
  397.1 5.7 fusion.46
  414.1 5.7 fusion.43
  427.4 5.7 fusion.46
  444.4 5.7 fusion.43
  457.8 5.7 fusion.46
  474.7 5.7 fusion.43
  488.1 5.7 fusion.46
  505.1 5.7 fusion.43
  518.4 5.7 fusion.46
  535.4 5.7 fusion.43
  548.8 5.7 fusion.46
  565.7 5.7 fusion.43
  579.1 5.7 fusion.46
  596.0 5.7 fusion.43
  609.4 5.7 fusion.46
  626.4 5.7 fusion.43
  639.8 5.7 fusion.46
  656.7 5.7 fusion.43
  687.0 5.7 fusion.43
  717.4 5.7 fusion.43
  738.9 5.8 fusion.23
  748.3 52.9 %reduce-scatter.4.cloned.1.call-done = bf16[640,320]{1,0:T(8,128)(2,1)} async-done(((bf16[5120,320]{1,0:T(8,128)(2,1)}), bf16[640,320]{1,0:T(8,128)(2,1)}) %reduce-scatter.4.cloned.1.call-update) | async-done | bytes 409616
  (367 shorter events, 316.5 us)
Async XLA Ops:
  6.5 14.0 %copy-start = (s32[16,16]{1,0:T(8,128)S(1)}, s32[16,16]{1,0:T(8,128)}, u32[]{:S(2)}) copy-start(s32[16,16]{1,0:T(8,128)} %param.10) | copy-start | bytes 3076
  6.5 12.7 %copy-start.2 = (bf16[1,4,80,640]{3,2,1,0:T(8,128)(2,1)S(1)}, bf16[1,4,80,640]{3,2,1,0:T(8,128)(2,1)}, u32[]{:S(2)}) copy-start(bf16[1,4,80,640]{3,2,1,0:T(8,128)(2,1)} %param.7) | copy-start | bytes 1228804
  6.5 245.4 %all-gather.2.cloned.1.call-start = ((), (), s32[]{:S(2)}) async-start(), calls=%async_computation.1 | async-start | bytes 41779200 | tf_op jit(solution)/shard_map/all_gather | solution.py:85
  7.8 6.5 collective-permute-start
  9.1 7.1 collective-permute-start.1
  19.1 782.1 %reduce-scatter.4.cloned.1.call-start = ((), (), s32[]{:S(2)}) async-start(), calls=%async_computation.2 | async-start | bytes 4423680
  275.9 5.5 copy-start.4
  281.4 3.7 copy-start.3
  306.1 5.7 copy-start.4
  311.8 3.7 copy-start.3
  336.4 5.7 copy-start.4
  342.1 3.7 copy-start.3
  366.8 5.7 copy-start.4
  372.4 3.7 copy-start.3
  397.1 5.7 copy-start.4
  402.8 3.7 copy-start.3
  427.4 5.7 copy-start.4
  433.1 3.7 copy-start.3
  457.8 5.7 copy-start.4
  488.1 5.7 copy-start.4
  493.8 3.7 copy-start.3
  518.4 5.7 copy-start.4
  548.8 5.7 copy-start.4
  554.4 3.7 copy-start.3
  579.1 5.7 copy-start.4
  609.4 5.7 copy-start.4
  639.8 5.7 copy-start.4
  670.1 5.7 copy-start.4
  700.4 5.7 copy-start.4
  706.1 3.7 copy-start.3
  730.8 5.7 copy-start.4
  738.9 64.3 %copy-start.1 = (s32[16,16]{1,0:T(8,128)S(1)}, s32[16,16]{1,0:T(8,128)}, u32[]{:S(2)}) copy-start(s32[16,16]{1,0:T(8,128)} %param.10) | copy-start | bytes 3076
  (7 other events, 26.2 us)
Sparse Core Ops, SparseCore 0:
  19.2 232.7 all-gather.1
  748.4 52.6 reduce-scatter.3
where the time goes:
time: 813 us; the launch traced here: 810 us
  waiting for transfers between devices  286 us (35%)
  matrix products  188 us (23%)
  other arithmetic  145 us (18%)
  local copies, waits for them, and re-layouts  141 us (17%)
  loops' own time  30.9 us (4%)
  between operations  13.5 us (2%)
    all_gather x1, waiting for transfers between devices, body(): piece = lax.all_gather(padded, 'tm', axis=1, tiled=True)  231 us
    dot_general x16, matrix products, absorb(): jnp.einsum('qhd,khd->hqk', queries, keys, preferred_element_type=jnp.floa...  91.6 us
    dot_general x16, matrix products, absorb(): jnp.einsum('hqk,khd->hqd', weights.astype(jnp.bfloat16), values, preferre...  90.3 us
    reduce_sum x16, other arithmetic, absorb(): new_sum = run_sum * factor + jnp.sum(weights, axis=-1)  78.2 us
    unnamed x3, waiting for transfers between devices  52.9 us
    squeeze x16, local copies, waits for them, and re-layouts, absorb_frame(): keys = kv_frame[0].reshape(span_rows * width, heads_dev, HD)  42.2 us
    another operation x1, loops' own time, body(): lax.scan(one_frame, empty_state(heads_dev, qcount), jnp.arange(piece.shap...  30.9 us
    slice x16, local copies, waits for them, and re-layouts, absorb_frame(): values = kv_frame[1].reshape(span_rows * width, heads_dev, HD)  30 us
  transfers between devices with their start and end apart: 4, of which 3 were waited for; matrix products, arithmetic and copies ran while one was open for 0% of the time, Pallas kernels for 0%

commit v1 on v0

--- a/solution.py
+++ b/solution.py
@@ -82,7 +82,9 @@
     key_rows = first_row - HALO + jnp.arange(rows_dev + 2 * HALO, dtype=jnp.int32)
     my_windows = lax.dynamic_slice_in_dim(window, first_frame, frames_dev, 0)
     queries = query.reshape(qcount, heads_dev, HD)
-    piece = lax.all_gather(padded, "tm", axis=1, tiled=True)
+    piece = jnp.concatenate(
+        lax.all_to_all(jnp.stack([padded] * lax.axis_size("tm")), "tm", 0, 0), axis=1
+    )
 
     def one_frame(carry, offset):
         kv_frame = lax.dynamic_index_in_dim(piece, offset, 1, False)

time: 813 us -> 1190 us (1.46)
  waiting for transfers between devices: 286 us -> 641 us
  local copies, waits for them, and re-layouts: 141 us -> 158 us
    all_to_all x0 -> x1, waiting for transfers between devices: none -> 588 us  [body(): lax.all_to_all(jnp.stack([padded] * lax.axis_size('tm')), 'tm', 0, 0)]
    all_gather x1 -> x0, waiting for transfers between devices: 231 us -> none  [body(): piece = lax.all_gather(padded, 'tm', axis=1, tiled=True)]
    dynamic_slice x0 -> x16, local copies, waits for them, and re-layouts: none -> 30.6 us  [one_frame(): kv_frame = lax.dynamic_index_in_dim(piece, offset, 1, False)]
    slice x16, local copies, waits for them, and re-layouts: 30 us -> 3.41 us  [absorb_frame(): values = kv_frame[1].reshape(span_rows * width, heads_dev, HD)]
    another operation x0 -> x1, local copies, waits for them, and re-layouts: none -> 13 us  [body(): jnp.stack([padded] * lax.axis_size('tm'))]
    unnamed x3 -> x2, waiting for transfers between devices: 52.9 us -> 50.5 us
where the time goes in v1:
time: 1190 us
  waiting for transfers between devices  641 us (54%)
  matrix products  188 us (16%)
  local copies, waits for them, and re-layouts  158 us (13%)
  other arithmetic  143 us (12%)
  loops' own time  28.8 us (2%)
  between operations  13.5 us (1%)
  starting transfers between devices  12.8 us (1%)
    all_to_all x1, waiting for transfers between devices, body(): lax.all_to_all(jnp.stack([padded] * lax.axis_size('tm')), 'tm', 0, 0)  588 us
    dot_general x16, matrix products, absorb(): jnp.einsum('qhd,khd->hqk', queries, keys, preferred_element_type=jnp.floa...  91.7 us
    dot_general x16, matrix products, absorb(): jnp.einsum('hqk,khd->hqd', weights.astype(jnp.bfloat16), values, preferre...  90.8 us
    reduce_sum x16, other arithmetic, absorb(): new_sum = run_sum * factor + jnp.sum(weights, axis=-1)  78.2 us
    unnamed x2, waiting for transfers between devices  50.5 us
    squeeze x16, local copies, waits for them, and re-layouts, absorb_frame(): keys = kv_frame[0].reshape(span_rows * width, heads_dev, HD)  42.7 us
    dynamic_slice x16, local copies, waits for them, and re-layouts, one_frame(): kv_frame = lax.dynamic_index_in_dim(piece, offset, 1, False)  30.6 us
    another operation x1, loops' own time, body(): lax.scan(one_frame, empty_state(heads_dev, qcount), jnp.arange(piece.shap...  28.8 us
  transfers between devices with their start and end apart: 4, of which 3 were waited for; matrix products, arithmetic and copies ran while one was open for 0% of the time, Pallas kernels for 0%

profile of v1, /device:TPU:1, one launch (start us, length us, event | category | flops | bytes accessed | tf_op | source)
XLA Modules:
  0.0 1185.1 jit_solution(3922289781178634507)
XLA Ops:
  17.6 13.0 %stack.11 = bf16[16,2,1,12,80,640]{5,4,3,1,2,0:T(8,128)(2,1)} broadcast(bf16[2,12,80,640]{3,2,1,0:T(8,128)(2,1)S(1)} %maximum_bitcast_fusion), dimensions={1,3,4,5} | broadcast | bytes 41779200 | tf_op jit(solution)/shard_map/stack | solution.py:86
  30.6 6.3 all-to-all-start
  38.8 588.4 %all-to-all-done = bf16[16,2,1,12,80,640]{5,4,3,1,2,0:T(8,128)(2,1)} async-done(((bf16[16,2,1,12,80,640]{5,4,3,1,2,0:T(8,128)(2,1)}), bf16[16,2,1,12,80,640]{5,4,3,1,2,0:T(8,128)(2,1)}, u32[]{:S(2)}, u32[]{:S(2)}) %all-to-all-start) | async-done | bytes 39321632 | tf_op jit(solution)/shard_map/all_to_all | solution.py:86
  627.3 486.7 %while.15 = (s32[]{:T(128)}, f32[5,320]{1,0:T(8,128)S(1)}, f32[5,320]{1,0:T(8,128)}, f32[5,320,128]{2,1,0:T(8,128)}, s32[16]{0:T(128)S(1)}, /*index=5*/s32[1,16]...) while((s32[]{:T(128)}, f32[5,320]{1,0:T(8,128)S(1)}, ...), condition=%wide.region_3.4_spmd.clone, body=%wide.region_0.3_spmd.clone.sunk | while | flops 803950720 | bytes 40244324 | solution.py:97
  638.6 5.7 fusion.46
  668.2 5.7 fusion.46
  681.6 5.7 fusion.49
  698.7 5.7 fusion.46
  712.1 5.7 fusion.49
  729.2 5.7 fusion.46
  742.6 5.7 fusion.49
  759.7 5.7 fusion.46
  773.1 5.7 fusion.49
  790.1 5.7 fusion.46
  803.5 5.7 fusion.49
  820.6 5.7 fusion.46
  834.0 5.7 fusion.49
  851.1 5.7 fusion.46
  864.5 5.7 fusion.49
  881.6 5.7 fusion.46
  894.9 5.7 fusion.49
  912.0 5.7 fusion.46
  925.4 5.7 fusion.49
  942.5 5.7 fusion.46
  955.9 5.7 fusion.49
  973.0 5.7 fusion.46
  1003.4 5.7 fusion.46
  1033.9 5.7 fusion.46
  1064.4 5.7 fusion.46
  1094.9 5.7 fusion.46
  1116.4 5.8 fusion.23
  1125.8 50.5 %reduce-scatter.4.cloned.1.call-done = bf16[640,320]{1,0:T(8,128)(2,1)} async-done(((bf16[5120,320]{1,0:T(8,128)(2,1)}), bf16[640,320]{1,0:T(8,128)(2,1)}) %reduce-scatter.4.cloned.1.call-update) | async-done | bytes 409616
  (383 shorter events, 330.3 us)
Async XLA Ops:
  6.5 31.8 %copy-start = (s32[16,16]{1,0:T(8,128)S(1)}, s32[16,16]{1,0:T(8,128)}, u32[]{:S(2)}) copy-start(s32[16,16]{1,0:T(8,128)} %param.10) | copy-start | bytes 3076
  7.8 6.5 collective-permute-start
  9.1 7.1 collective-permute-start.1
  30.6 6.4 copy-start.2
  30.6 596.7 %all-to-all-start = ((bf16[16,2,1,12,80,640]{5,4,3,1,2,0:T(8,128)(2,1)}), bf16[16,2,1,12,80,640]{5,4,3,1,2,0:T(8,128)(2,1)}, u32[]{:S(2)}, u32[]{:S(2)}) async-start(bf16[16,2,1,12,80,640]{5,4,3,1,2,0:T(8,128)(2,1)} %stack.11), calls=%async_computation | async-start | bytes 78643200 | tf_op jit(solution)/shard_map/all_to_all | solution.py:86
  36.9 1139.4 %reduce-scatter.4.cloned.1.call-start = ((), (), s32[]{:S(2)}) async-start(), calls=%async_computation.2 | async-start | bytes 4423680
  651.3 5.5 copy-start.4
  656.9 3.5 copy-start.3
  681.6 5.7 copy-start.4
  687.3 3.5 copy-start.3
  712.1 5.7 copy-start.4
  717.8 3.5 copy-start.3
  742.6 5.7 copy-start.4
  748.3 3.5 copy-start.3
  773.1 5.7 copy-start.4
  778.8 3.5 copy-start.3
  803.5 5.7 copy-start.4
  834.0 5.7 copy-start.4
  864.5 5.7 copy-start.4
  894.9 5.7 copy-start.4
  925.4 5.7 copy-start.4
  955.9 5.7 copy-start.4
  986.4 5.7 copy-start.4
  992.1 3.5 copy-start.3
  1016.8 5.7 copy-start.4
  1022.5 3.5 copy-start.3
  1047.3 5.7 copy-start.4
  1053.0 3.5 copy-start.3
  1077.8 5.7 copy-start.4
  1083.5 3.5 copy-start.3
  1108.2 5.7 copy-start.4
  1122.2 56.1 %copy-start.1 = (s32[16,16]{1,0:T(8,128)S(1)}, s32[16,16]{1,0:T(8,128)}, u32[]{:S(2)}) copy-start(s32[16,16]{1,0:T(8,128)} %param.10) | copy-start | bytes 3076
  (7 other events, 24.8 us)
Sparse Core Ops, SparseCore 0:
  1126.0 50.2 reduce-scatter.3
